TPU v7x, 128 devices: a whole 4x4x4 slice. The times are simulated.
128 devices in a mesh: sph: 16 (over y_hi, x, core), grp: 8 (over z, y_lo).
Axes of the slice: x: 4, y: 4 (y_hi: 2, y_lo: 2; y = y_hi * 2 + y_lo), z: 4, core: 2. Of those that a mesh axis runs over, the one named last changes fastest.
Arguments:
- pixel_features: bfloat16 [131072, 512], P(('sph', 'grp')), may hold values from -6 to 6
- tier_one_codes: bfloat16 [8192, 512], P(('sph', 'grp')), may hold values from -6 to 6
- tier_two_codes: bfloat16 [512, 512], P(('sph', 'grp')), may hold values from -6 to 6
- tier_three_codes: bfloat16 [32, 512], P('sph'), may hold values from -6 to 6
- tier_one_picks: int32 [8192, 16], P(('sph', 'grp')), may hold values from 0 to 8191, as said below
- tier_two_picks: int32 [8192, 16], P(('sph', 'grp')), may hold values from 0 to 511, as said below
- tier_three_picks: int32 [8192, 16], P(('sph', 'grp')), may hold values from 0 to 31, as said below
- probe_matrix: bfloat16 [3, 512, 512], replicated, may hold values from -0.25 to 0.25
- address_matrix: bfloat16 [3, 512, 512], replicated, may hold values from -0.25 to 0.25
- content_matrix: bfloat16 [3, 512, 512], replicated, may hold values from -0.25 to 0.25
- merge_matrix: bfloat16 [3, 512, 512], replicated, may hold values from -0.25 to 0.25
- expand_matrix: bfloat16 [3, 512, 1024], replicated, may hold values from -0.25 to 0.25
- shrink_matrix: bfloat16 [3, 1024, 512], replicated, may hold values from -0.1875 to 0.1875
- rescale_factors: float32 [3, 3, 512], replicated, may hold values from 0.25 to 1.75
- logit_scaling: float32 [3, 8], replicated, may hold values from 0.5 to 2
Outputs:
- encoded: bfloat16 [131072, 512], P(('sph', 'grp'))
Inputs may be any that keep to these rules, and one draw needn't show every extreme that they name: `tier_one_picks`: entry 0 of block b's list is b, its own level-one parent; every entry lies within 64 of b. `tier_two_picks`: entry 0 of block b's list is b // 16, its level-two parent; every entry lies in the same aligned run of 32 level-two latents as entry 0. `tier_three_picks`: entry 0 of block b's list is b // 256, its level-three parent.
All inputs are finite; a program needn't handle non-finite values.
Results may differ from a plain program's by a relative error of at most 0.01.
Values may be sent and summed in bfloat16 or wider, within the bound.
No kernel may reach another device: no remote copies, remote signals or barrier semaphores. Data moves between devices by JAX's collectives and lax.ppermute only.
A program may use at most 128 MiB of HBM per device.

v0:
```python
import math
import jax
import jax.numpy as jnp
from jax import lax
from jax.sharding import PartitionSpec as P

eps = 1e-06


def with_halo(block, sides, width):
    for axis, dim in sides:
        count = lax.axis_size(axis)
        forward = [(i, i + 1) for i in range(count - 1)]
        backward = [(target, source) for source, target in forward]
        low = lax.ppermute(
            lax.slice_in_dim(block, block.shape[dim] - width, None, axis=dim), axis, forward
        )
        high = lax.ppermute(lax.slice_in_dim(block, 0, width, axis=dim), axis, backward)
        block = jnp.concatenate([low, block, high], axis=dim)
    return block


def normalize(values_in, gain_vec):
    return (
        values_in
        * lax.rsqrt(jnp.mean(values_in * values_in, axis=-1, keepdims=True) + eps)
        * gain_vec
    )


def per_head(values_in, channel_groups):
    dims_shape = values_in.shape
    grouped = values_in.reshape(
        dims_shape[:-1] + (channel_groups, dims_shape[-1] // channel_groups)
    )
    grouped = grouped * lax.rsqrt(jnp.mean(grouped * grouped, axis=-1, keepdims=True) + eps)
    return grouped.reshape(dims_shape)


def refresh(latent, tier_ordinal, expand_matrix, shrink_matrix, rescale_factors):
    running_features = latent.astype(jnp.float32)
    mlp_in = normalize(running_features, rescale_factors[tier_ordinal, 1]).astype(jnp.bfloat16)
    hidden = jax.nn.silu(
        jnp.dot(mlp_in, expand_matrix[tier_ordinal], preferred_element_type=jnp.float32)
    ).astype(jnp.bfloat16)
    renewed = (
        running_features
        + jnp.dot(hidden, shrink_matrix[tier_ordinal], preferred_element_type=jnp.float32)
    ).astype(jnp.bfloat16)
    return lax.optimization_barrier(renewed)


def project(renewed, tier_ordinal, address_matrix, content_matrix, rescale_factors, channel_groups):
    kv_in = normalize(renewed.astype(jnp.float32), rescale_factors[tier_ordinal, 2]).astype(
        jnp.bfloat16
    )
    key_part = per_head(
        jnp.dot(kv_in, address_matrix[tier_ordinal], preferred_element_type=jnp.float32),
        channel_groups,
    ).astype(jnp.bfloat16)
    value_part = jnp.dot(
        kv_in, content_matrix[tier_ordinal], preferred_element_type=jnp.float32
    ).astype(jnp.bfloat16)
    return jnp.concatenate([key_part, value_part], axis=1)


def mix_across_tiers(
    running_features,
    gather_entries,
    tier_positions,
    tier_ordinal,
    probe_matrix,
    merge_matrix,
    rescale_factors,
    logit_scaling,
):
    row_count, feature = running_features.shape
    blocks = tier_positions.shape[0]
    channel_groups = logit_scaling.shape[1]
    group_dimension = feature // channel_groups
    table_rows = gather_entries.shape[0]
    normed = normalize(running_features, rescale_factors[tier_ordinal, 0]).astype(jnp.bfloat16)
    probe_heads = probe_matrix[tier_ordinal].reshape(feature, channel_groups, group_dimension)
    queries = jnp.einsum("rc,chd->hrd", normed, probe_heads, preferred_element_type=jnp.float32)
    queries = queries * lax.rsqrt(jnp.mean(queries * queries, axis=-1, keepdims=True) + eps)
    queries = queries.astype(jnp.bfloat16).reshape(
        channel_groups, blocks, row_count // blocks, group_dimension
    )
    key_heads = jnp.transpose(
        gather_entries[:, :feature].reshape(table_rows, channel_groups, group_dimension), (1, 0, 2)
    )
    value_heads = jnp.transpose(
        gather_entries[:, feature:].reshape(table_rows, channel_groups, group_dimension), (1, 0, 2)
    )
    key_picked = jnp.take(key_heads, tier_positions, axis=1)
    value_picked = jnp.take(value_heads, tier_positions, axis=1)
    affinity_logits = jnp.einsum(
        "hbid,hbjd->hbij", queries, key_picked, preferred_element_type=jnp.float32
    )
    affinity_logits = (
        affinity_logits
        * (logit_scaling[tier_ordinal] / math.sqrt(group_dimension))[:, None, None, None]
    )
    weights = jnp.exp(affinity_logits)
    weights = (weights / jnp.sum(weights, axis=-1, keepdims=True)).astype(jnp.bfloat16)
    mixture = jnp.einsum(
        "hbij,hbjd->hbid", weights, value_picked, preferred_element_type=jnp.float32
    )
    mixture = mixture.astype(jnp.bfloat16).reshape(channel_groups, row_count, group_dimension)
    merge_heads = merge_matrix[tier_ordinal].reshape(channel_groups, group_dimension, feature)
    return running_features + jnp.einsum(
        "hrd,hde->re", mixture, merge_heads, preferred_element_type=jnp.float32
    )


def per_device(
    pixel_features,
    tier_one_codes,
    tier_two_codes,
    tier_three_codes,
    tier_one_picks,
    tier_two_picks,
    tier_three_picks,
    probe_matrix,
    address_matrix,
    content_matrix,
    merge_matrix,
    expand_matrix,
    shrink_matrix,
    rescale_factors,
    logit_scaling,
):
    channel_groups = logit_scaling.shape[1]
    block_count = tier_one_codes.shape[0]
    device_index = lax.axis_index(("sph", "grp"))
    sphere_index = lax.axis_index("sph")
    renewed_one = refresh(tier_one_codes, 0, expand_matrix, shrink_matrix, rescale_factors)
    renewed_two = refresh(tier_two_codes, 1, expand_matrix, shrink_matrix, rescale_factors)
    renewed_three = refresh(tier_three_codes, 2, expand_matrix, shrink_matrix, rescale_factors)
    first_table = with_halo(
        project(renewed_one, 0, address_matrix, content_matrix, rescale_factors, channel_groups),
        ((("sph", "grp"), 0),),
        block_count,
    )
    second_table = lax.all_gather(
        project(renewed_two, 1, address_matrix, content_matrix, rescale_factors, channel_groups),
        "grp",
        axis=0,
        tiled=True,
    )
    third_table = lax.all_gather(
        project(renewed_three, 2, address_matrix, content_matrix, rescale_factors, channel_groups),
        "sph",
        axis=0,
        tiled=True,
    )
    local_first = tier_one_picks - (device_index * block_count - block_count)
    local_second = tier_two_picks - sphere_index * second_table.shape[0]
    running_features = pixel_features.astype(jnp.float32)
    running_features = mix_across_tiers(
        running_features,
        first_table,
        local_first,
        0,
        probe_matrix,
        merge_matrix,
        rescale_factors,
        logit_scaling,
    )
    running_features = mix_across_tiers(
        running_features,
        second_table,
        local_second,
        1,
        probe_matrix,
        merge_matrix,
        rescale_factors,
        logit_scaling,
    )
    running_features = mix_across_tiers(
        running_features,
        third_table,
        tier_three_picks,
        2,
        probe_matrix,
        merge_matrix,
        rescale_factors,
        logit_scaling,
    )
    return running_features.astype(jnp.bfloat16)


def solution(mesh):
    placed = (
        P(("sph", "grp"), None),
        P(("sph", "grp"), None),
        P(("sph", "grp"), None),
        P("sph", None),
        P(("sph", "grp"), None),
        P(("sph", "grp"), None),
        P(("sph", "grp"), None),
        P(),
        P(),
        P(),
        P(),
        P(),
        P(),
        P(),
        P(),
    )
    return jax.shard_map(
        per_device, mesh=mesh, in_specs=placed, out_specs=P(("sph", "grp"), None), check_vma=False
    )
```

profile of v0, /device:TPU:1, one launch (start us, length us, event | category | flops | bytes accessed | tf_op | source)
XLA Modules:
  0.0 174.7 jit_solution(10570810775063675648)
XLA Ops:
  2.5 2.1 %fusion.35 = bf16[64,512]{1,0:T(8,128)(2,1)S(1)} fusion(bf16[3,1024,512]{2,1,0:T(8,128)(2,1)} %param.31, bf16[3,512,1024]{2,1,0:T(8,128)(2,1)} %param.30, bf16[64,512]{1,0:T(8,128)(2,1)} %param.20, f32[512]{0:T(512)S(1)} %bitcast.234, f32[64]{0:T(128)S(1)} %add_rsqrt_fusion.14), kind=kOutput, calls=%fused_computation.63 | convolution fusion | flops 134774784 | bytes 2296064 | tf_op jit(solution)/shard_map/dot_general | solution.py:48
  7.9 4.0 %collective-permute-start = (bf16[64,1024]{1,0:T(8,128)(2,1)S(1)}, bf16[64,1024]{1,0:T(8,128)(2,1)S(1)}, u32[]{:S(2)}, u32[]{:S(2)}) collective-permute-start(bf16[64,1024]{1,0:T(8,128)(2,1)S(1)} %pad_maximum_fusion.1), channel_id=1, source_target_pairs={{0,1},{1,2},{2,3},{3,4},{4,5},{5,6},{6,7},{7,8},{8,9},{9,10},{10,1... | collective-permute-start | bytes 393224 | tf_op jit(solution)/shard_map/ppermute | solution.py:15
  11.9 6.0 %collective-permute-start.1 = (bf16[64,1024]{1,0:T(8,128)(2,1)S(1)}, bf16[64,1024]{1,0:T(8,128)(2,1)}, u32[]{:S(2)}, u32[]{:S(2)}) collective-permute-start(bf16[64,1024]{1,0:T(8,128)(2,1)S(1)} %pad_maximum_fusion.1), channel_id=1, source_target_pairs={{1,0},{2,1},{3,2},{4,3},{5,4},{6,5},{7,6},{8,7},{9,8},{10,9},{11,1... | collective-permute-start | bytes 393224 | tf_op jit(solution)/shard_map/ppermute | solution.py:18
  20.2 1.9 %multiply_reduce_fusion.4 = (f32[8,1024]{1,0:T(8,128)S(1)}, f32[1024,512]{0,1:S(1)}) fusion(bf16[1024,512]{0,1:T(8,128)(2,1)S(1)} %copy.136, f32[512]{0:T(512)S(1)} %bitcast.233, f32[1024]{0:T(1024)S(1)} %add_rsqrt_fusion.8, bf16[3,512,512]{2,1,0:T(8,128)(2,1)} %param.26), kind=kOutput, calls=%fused_computation.54 | convolution fusion | flops 540008448 | bytes 3708928
  23.6 2.7 %fusion.155 = (bf16[1,512,512]{2,1,0:T(8,128)(2,1)}, bf16[1,512,512]{2,1,0:T(8,128)(2,1)}, bf16[1,512,512]{2,1,0:T(8,128)(2,1)}) fusion(bf16[3,512,512]{2,1,0:T(8,128)(2,1)} %param.29), kind=kLoop, calls=%fused_computation.208 | loop fusion | bytes 3145728 | tf_op jit(solution)/shard_map/slice | solution.py:110
  26.4 2.0 %fusion.36 = bf16[4,512]{1,0:T(4,128)(2,1)S(1)} fusion(bf16[3,1024,512]{2,1,0:T(8,128)(2,1)} %param.31, bf16[3,512,1024]{2,1,0:T(8,128)(2,1)} %param.30, bf16[4,512]{1,0:T(4,128)(2,1)S(1)} %copy-done.21, f32[512]{0:T(512)S(1)} %bitcast.232, f32[4]{0:T(128)S(1)} %add_rsqrt_fusion.12), kind=kOutput, calls=%fused_computation.66 | convolution fusion | flops 8423424 | bytes 2112000 | tf_op jit(solution)/shard_map/dot_general | solution.py:48
  31.8 22.1 %all-gather = bf16[8,4,1024]{2,1,0:T(4,128)(2,1)S(1)} all-gather(bf16[1,4,1024]{2,1,0:T(4,128)(2,1)S(1)} %maximum_bitcast_fusion), channel_id=1, replica_groups=mesh['sph'=16,'grp'=8] {'grp'}, dimensions={0}, use_global_device_ids=true | all-gather | bytes 73728 | tf_op jit(solution)/shard_map/all_gather | solution.py:145
  55.7 7.6 %gather_fusion.2 = bf16[1024,8,64]{2,1,0:T(8,128)(2,1)} fusion(bf16[8,32,64]{2,0,1:T(8,128)(2,1)S(1)} %bitcast.199, s32[1024]{0:T(1024)S(1)} %broadcast_clamp_fusion.1), kind=kCustom, calls=%fused_computation.1.clone | custom fusion | bytes 2101248 | tf_op jit(solution)/shard_map/jit(_take)/gather | solution.py:95
  63.4 7.6 %gather_fusion.3 = bf16[1024,8,64]{2,1,0:T(8,128)(2,1)} fusion(bf16[8,32,64]{2,0,1:T(8,128)(2,1)S(1)} %bitcast.201, s32[1024]{0:T(1024)S(1)} %broadcast_clamp_fusion.1), kind=kCustom, calls=%fused_computation.3.clone | custom fusion | bytes 2101248 | tf_op jit(solution)/shard_map/jit(_take)/gather | solution.py:96
  71.1 2.0 %fusion.37 = bf16[2,512]{1,0:T(2,128)(2,1)S(1)} fusion(bf16[3,1024,512]{2,1,0:T(8,128)(2,1)} %param.31, bf16[3,512,1024]{2,1,0:T(8,128)(2,1)} %param.30, bf16[2,512]{1,0:T(2,128)(2,1)S(1)} %copy-done.24, f32[2]{0:T(128)S(1)} %add_rsqrt_fusion.10, f32[512]{0:T(512)S(1)} %bitcast.231), kind=kOutput, calls=%fused_computation.69 | convolution fusion | flops 4211712 | bytes 2105856 | tf_op jit(solution)/shard_map/dot_general | solution.py:48
  76.5 30.7 %all-gather.1 = bf16[16,2,1024]{2,1,0:T(2,128)(2,1)S(1)} all-gather(bf16[1,2,1024]{2,1,0:T(2,128)(2,1)S(1)} %maximum_bitcast_fusion.1), channel_id=1, replica_groups=mesh['sph'=16,'grp'=8] {'sph'}, dimensions={0}, use_global_device_ids=true | all-gather | bytes 69632 | tf_op jit(solution)/shard_map/all_gather | solution.py:151
  109.7 7.6 %gather_fusion.4 = bf16[1024,8,64]{2,1,0:T(8,128)(2,1)} fusion(bf16[8,32,64]{2,0,1:T(8,128)(2,1)S(1)} %bitcast.200, s32[1024]{0:T(1024)S(1)} %broadcast_clamp_fusion), kind=kCustom, calls=%fused_computation.4.clone | custom fusion | bytes 2101248 | tf_op jit(solution)/shard_map/jit(_take)/gather | solution.py:95
  117.3 7.6 %gather_fusion.5 = bf16[1024,8,64]{2,1,0:T(8,128)(2,1)} fusion(bf16[8,32,64]{2,0,1:T(8,128)(2,1)S(1)} %bitcast.202, s32[1024]{0:T(1024)S(1)} %broadcast_clamp_fusion), kind=kCustom, calls=%fused_computation.5.clone | custom fusion | bytes 2101248 | tf_op jit(solution)/shard_map/jit(_take)/gather | solution.py:96
  127.2 7.6 %gather_fusion.1 = bf16[1024,8,64]{2,1,0:T(8,128)(2,1)} fusion(bf16[8,192,64]{2,0,1:T(8,128)(2,1)S(1)} %bitcast.203, s32[1024]{0:T(1024)S(1)} %broadcast_clamp_fusion.2), kind=kCustom, calls=%fused_computation.2.clone | custom fusion | bytes 2101248 | tf_op jit(solution)/shard_map/jit(_take)/gather | solution.py:96
  134.8 7.6 %gather_fusion = bf16[1024,8,64]{2,1,0:T(8,128)(2,1)} fusion(bf16[8,192,64]{2,0,1:T(8,128)(2,1)S(1)} %bitcast.204, s32[1024]{0:T(1024)S(1)} %broadcast_clamp_fusion.2), kind=kCustom, calls=%fused_computation.clone | custom fusion | bytes 2101248 | tf_op jit(solution)/shard_map/jit(_take)/gather | solution.py:95
  142.5 3.5 %select_bitcast_fusion.1 = (bf16[8,64,16,64]{3,0,2,1:T(8,128)(2,1)S(1)}, bf16[8,64,16,64]{3,0,2,1:T(8,128)(2,1)S(1)}) fusion(bf16[64,16,8,64]{3,2,1,0:T(8,128)(2,1)} %bitcast.207, pred[64,16]{1,0:T(8,128)(4,1)S(1)} %copy.140, bf16[64,16,8,64]{3,2,1,0:T(8,128)(2,1)} %bitcast.206), kind=kLoop, calls=%fused_computation.41 | loop fusion | flops 1048576 | bytes 4195328 | tf_op jit(solution)/shard_map/jit(_take)/select_n | solution.py:95
  147.5 1.6 fusion.26
  150.5 2.3 %multiply_reduce_fusion.2 = (f32[8,1024]{1,0:T(8,128)S(1)}, f32[1024,512]{0,1:S(1)}) fusion(f32[1024,512]{0,1:T(8,128)S(1)} %get-tuple-element.46, f32[512]{0:T(512)S(1)} %bitcast.224, f32[1024]{0:T(1024)S(1)} %add_rsqrt_fusion.6, bf16[3,512,512]{2,1,0:T(8,128)(2,1)} %param.26), kind=kOutput, calls=%fused_computation.49 | convolution fusion | flops 539484160 | bytes 4757504
  154.2 4.3 %fusion.1 = (f32[8,64,16]{2,1,0:T(8,128)S(1)}, f32[8,64,16,16]{2,3,1,0:T(8,128)S(1)}) fusion(f32[8]{0:T(128)S(1)} %copy-done.27, bf16[8,64,16,64]{3,2,1,0:T(8,128)(2,1)S(1)} %bitcast.209, bf16[64,16,8,64]{3,2,1,0:T(8,128)(2,1)} %bitcast.212, pred[64,16]{1,0:T(8,128)(4,1)S(1)} %copy-done.19), kind=kOutput, calls=%fused_computation.13 | convolution fusion | flops 17555456 | bytes 2655264 | tf_op jit(solution)/shard_map/hbid,hbjd->hbij/dot_general | solution.py:97
  158.6 2.1 %fusion.29 = bf16[8,64,16,64]{3,2,1,0:T(8,128)(2,1)S(1)} fusion(bf16[64,16,8,64]{3,2,1,0:T(8,128)(2,1)S(1)} %bitcast.211, pred[64,16]{1,0:T(8,128)(4,1)S(1)} %copy-done.19, f32[8,64,16,16]{2,3,1,0:T(8,128)S(1)} %get-tuple-element.50, f32[8,64,16]{2,1,0:T(8,128)S(1)} %get-tuple-element.49, f32[8]{0:T(128)S(1)} %copy-done.27), kind=kOutput, calls=%fused_computation.60 | convolution fusion | flops 18219008 | bytes 2655264 | tf_op jit(solution)/shard_map/hbij,hbjd->hbid/dot_general | solution.py:106
  162.1 1.9 %multiply_reduce_fusion = (f32[8,1024]{1,0:T(8,128)S(1)}, f32[1024,512]{0,1:S(1)}) fusion(f32[1024,512]{0,1:T(8,128)S(1)} %get-tuple-element.54, f32[512]{0:T(512)S(1)} %bitcast.223, f32[1024]{0:T(1024)S(1)} %add_rsqrt_fusion.4, bf16[3,512,512]{2,1,0:T(8,128)(2,1)} %param.26), kind=kOutput, calls=%fused_computation.44 | convolution fusion | flops 539484160 | bytes 4757504
  164.2 1.8 %copy.169 = bf16[8,1024,64]{2,1,0:T(8,128)(2,1)} copy(bf16[8,1024,64]{1,2,0:T(8,128)(2,1)S(1)} %multiply_convert_fusion) | data formatting | bytes 2097152 | tf_op jit(solution)/shard_map/convert_element_type | solution.py:86
  166.1 3.9 %fusion.2 = (f32[8,64,16]{2,1,0:T(8,128)S(1)}, f32[8,64,16,16]{2,3,1,0:T(8,128)S(1)}) fusion(f32[8]{0:T(128)S(1)} %copy-done.26, bf16[8,64,16,64]{3,2,1,0:T(8,128)(2,1)} %bitcast.208, bf16[64,16,8,64]{3,2,1,0:T(8,128)(2,1)} %bitcast.214, pred[64,16]{1,0:T(8,128)(4,1)S(1)} %copy-done.20), kind=kOutput, calls=%fused_computation.14 | convolution fusion | flops 17555456 | bytes 2655264 | tf_op jit(solution)/shard_map/hbid,hbjd->hbij/dot_general | solution.py:97
  170.0 2.1 %fusion.32 = bf16[8,64,16,64]{3,2,1,0:T(8,128)(2,1)S(1)} fusion(bf16[64,16,8,64]{3,2,1,0:T(8,128)(2,1)S(1)} %bitcast.213, pred[64,16]{1,0:T(8,128)(4,1)S(1)} %copy-done.20, f32[8,64,16,16]{2,3,1,0:T(8,128)S(1)} %get-tuple-element.58, f32[8,64,16]{2,1,0:T(8,128)S(1)} %get-tuple-element.57, f32[8]{0:T(128)S(1)} %copy-done.26), kind=kOutput, calls=%fused_computation.61 | convolution fusion | flops 18219008 | bytes 2655264 | tf_op jit(solution)/shard_map/hbij,hbjd->hbid/dot_general | solution.py:106
  (144 shorter events, 31.4 us)
Async XLA Ops:
  0.0 4.8 %copy-start.8 = (bf16[3,512,512]{2,1,0:T(8,128)(2,1)S(1)}, bf16[3,512,512]{2,1,0:T(8,128)(2,1)}, u32[]{:S(2)}) copy-start(bf16[3,512,512]{2,1,0:T(8,128)(2,1)} %param.27) | copy-start | bytes 4718596
  5.9 12.1 %copy-start.13 = (s32[64,16]{0,1:T(8,128)S(1)}, s32[64,16]{0,1:T(8,128)}, u32[]{:S(2)}) copy-start(s32[64,16]{0,1:T(8,128)} %param.25) | copy-start | bytes 12292
  5.9 13.2 %copy-start.18 = (s32[64,16]{0,1:T(8,128)S(1)}, s32[64,16]{0,1:T(8,128)}, u32[]{:S(2)}) copy-start(s32[64,16]{0,1:T(8,128)} %param.23) | copy-start | bytes 12292
  5.9 13.5 %copy-start.9 = (bf16[1024,512]{1,0:T(8,128)(2,1)S(1)}, bf16[1024,512]{1,0:T(8,128)(2,1)}, u32[]{:S(2)}) copy-start(bf16[1024,512]{1,0:T(8,128)(2,1)} %param.19) | copy-start | bytes 3145732
  7.9 117.6 %collective-permute-start = (bf16[64,1024]{1,0:T(8,128)(2,1)S(1)}, bf16[64,1024]{1,0:T(8,128)(2,1)S(1)}, u32[]{:S(2)}, u32[]{:S(2)}) collective-permute-start(bf16[64,1024]{1,0:T(8,128)(2,1)S(1)} %pad_maximum_fusion.1), channel_id=1, source_target_pairs={{0,1},{1,2},{2,3},{3,4},{4,5},{5,6},{6,7},{7,8},{8,9},{9,10},{10,1... | collective-permute-start | bytes 393224 | tf_op jit(solution)/shard_map/ppermute | solution.py:15
  11.9 113.5 %collective-permute-start.1 = (bf16[64,1024]{1,0:T(8,128)(2,1)S(1)}, bf16[64,1024]{1,0:T(8,128)(2,1)}, u32[]{:S(2)}, u32[]{:S(2)}) collective-permute-start(bf16[64,1024]{1,0:T(8,128)(2,1)S(1)} %pad_maximum_fusion.1), channel_id=1, source_target_pairs={{1,0},{2,1},{3,2},{4,3},{5,4},{6,5},{7,6},{8,7},{9,8},{10,9},{11,1... | collective-permute-start | bytes 393224 | tf_op jit(solution)/shard_map/ppermute | solution.py:18
  19.9 2.2 %copy-start = (bf16[1024,512]{0,1:T(8,128)(2,1)}, bf16[1024,512]{0,1:T(8,128)(2,1)S(1)}, u32[]{:S(2)}) copy-start(bf16[1024,512]{0,1:T(8,128)(2,1)S(1)} %copy.136) | copy-start | bytes 3145732
  23.5 2.7 %copy-start.21 = (bf16[4,512]{1,0:T(4,128)(2,1)S(1)}, bf16[4,512]{1,0:T(4,128)(2,1)}, u32[]{:S(2)}) copy-start(bf16[4,512]{1,0:T(4,128)(2,1)} %param.21) | copy-start | bytes 12292
  23.6 2.8 %copy-start.23 = (f32[1,1,512]{2,1,0:T(1,128)S(1)}, f32[1,1,512]{2,1,0:T(1,128)}, u32[]{:S(2)}) copy-start(f32[1,1,512]{2,1,0:T(1,128)} %get-tuple-element.25) | copy-start | bytes 6148
  23.6 5.4 %copy-start.7 = (bf16[512,512]{0,1:T(8,128)(2,1)S(1)}, bf16[512,512]{0,1:T(8,128)(2,1)}, u32[]{:S(2)}) copy-start(bf16[512,512]{0,1:T(8,128)(2,1)} %get-tuple-element.16) | copy-start | bytes 1572868
  63.4 7.6 %copy-start.24 = (bf16[2,512]{1,0:T(2,128)(2,1)S(1)}, bf16[2,512]{1,0:T(2,128)(2,1)}, u32[]{:S(2)}) copy-start(bf16[2,512]{1,0:T(2,128)(2,1)} %param.22) | copy-start | bytes 6148
  63.4 7.7 %copy-start.22 = (f32[1,1,512]{2,1,0:T(1,128)S(1)}, f32[1,1,512]{2,1,0:T(1,128)}, u32[]{:S(2)}) copy-start(f32[1,1,512]{2,1,0:T(1,128)} %get-tuple-element.31) | copy-start | bytes 6148
  71.0 2.8 %copy-start.6 = (bf16[512,512]{0,1:T(8,128)(2,1)S(1)}, bf16[512,512]{0,1:T(8,128)(2,1)}, u32[]{:S(2)}) copy-start(bf16[512,512]{0,1:T(8,128)(2,1)} %get-tuple-element.14) | copy-start | bytes 1572868
  71.0 3.0 %copy-start.16 = (f32[1,1,512]{2,1,0:T(1,128)S(1)}, f32[1,1,512]{2,1,0:T(1,128)}, u32[]{:S(2)}) copy-start(f32[1,1,512]{2,1,0:T(1,128)} %get-tuple-element.30) | copy-start | bytes 6148
  117.3 7.6 %copy-start.25 = (f32[3,8]{1,0:T(4,128)S(1)}, f32[3,8]{1,0:T(4,128)}, u32[]{:S(2)}) copy-start(f32[3,8]{1,0:T(4,128)} %param.33) | copy-start | bytes 292
  147.4 1.7 copy-start.1
  150.5 2.3 %copy-start.2 = (f32[1024,512]{0,1:T(8,128)}, f32[1024,512]{0,1:T(8,128)S(1)}, u32[]{:S(2)}) copy-start(f32[1024,512]{0,1:T(8,128)S(1)} %get-tuple-element.46) | copy-start | bytes 6291460
  154.2 4.3 %copy-start.4 = (bf16[1024,8,64]{2,1,0:T(8,128)(2,1)S(1)}, bf16[1024,8,64]{2,1,0:T(8,128)(2,1)}, u32[]{:S(2)}) copy-start(bf16[1024,8,64]{2,1,0:T(8,128)(2,1)} %gather_fusion.3) | copy-start | bytes 3145732
  158.6 2.1 %copy-start.3 = (f32[1024,512]{0,1:T(8,128)S(1)}, f32[1024,512]{0,1:T(8,128)}, u32[]{:S(2)}) copy-start(f32[1024,512]{0,1:T(8,128)} %copy-done.2) | copy-start | bytes 6291460
  158.6 2.1 %copy-start.11 = (bf16[1,512,512]{2,1,0:T(8,128)(2,1)S(1)}, bf16[1,512,512]{2,1,0:T(8,128)(2,1)}, u32[]{:S(2)}) copy-start(bf16[1,512,512]{2,1,0:T(8,128)(2,1)} %get-tuple-element.13) | copy-start | bytes 1572868
  164.2 1.9 %copy-start.20 = (pred[64,16]{1,0:T(8,128)(4,1)S(1)}, pred[64,16]{1,0:T(8,128)(4,1)}, u32[]{:S(2)}) copy-start(pred[64,16]{1,0:T(8,128)(4,1)} %copy.170) | copy-start | bytes 3076
  164.2 1.8 %copy-start.26 = (f32[8]{0:T(128)S(1)}, f32[8]{0:T(128)}, u32[]{:S(2)}) copy-start(f32[8]{0:T(128)} %get-tuple-element.34) | copy-start | bytes 100
  166.1 3.9 %copy-start.5 = (bf16[1024,8,64]{2,1,0:T(8,128)(2,1)S(1)}, bf16[1024,8,64]{2,1,0:T(8,128)(2,1)}, u32[]{:S(2)}) copy-start(bf16[1024,8,64]{2,1,0:T(8,128)(2,1)} %gather_fusion.5) | copy-start | bytes 3145732
  170.0 2.1 %copy-start.10 = (bf16[1,512,512]{2,1,0:T(8,128)(2,1)S(1)}, bf16[1,512,512]{2,1,0:T(8,128)(2,1)}, u32[]{:S(2)}) copy-start(bf16[1,512,512]{2,1,0:T(8,128)(2,1)} %get-tuple-element.11) | copy-start | bytes 1572868
  (6 other events, 7.3 us)
where the time goes:
time: 176 us; the launch traced here: 175 us
  local copies, waits for them, and re-layouts  62.3 us (35%)
  blocking collectives  52.8 us (30%)
  matrix products  37.9 us (22%)
  other arithmetic  11 us (6%)
  starting transfers between devices  9.98 us (6%)
    all_gather x1, blocking collectives, per_device(): lax.all_gather(project(renewed_three, 2, address_matrix, content_matrix,...  30.7 us
    gather x3, local copies, waits for them, and re-layouts, mix_across_tiers(): key_picked = jnp.take(key_heads, tier_positions, axis=1)  22.8 us
    gather x3, local copies, waits for them, and re-layouts, mix_across_tiers(): value_picked = jnp.take(value_heads, tier_positions, axis=1)  22.8 us
    all_gather x1, blocking collectives, per_device(): lax.all_gather(project(renewed_two, 1, address_matrix, content_matrix, re...  22.1 us
    dot_general x3, matrix products, mix_across_tiers(): jnp.einsum('hbid,hbjd->hbij', queries, key_picked, preferred_element_type...  9.67 us
    dot_general x3, matrix products, refresh(): jnp.dot(hidden, shrink_matrix[tier_ordinal], preferred_element_type=jnp.f...  6.09 us
    unnamed x3, matrix products  6.07 us
    ppermute x1, starting transfers between devices, with_halo(): lax.ppermute(lax.slice_in_dim(block, 0, width, axis=dim), axis, backward)  5.96 us
  transfers between devices with their start and end apart: 2, of which 0 were waited for; matrix products, arithmetic and copies ran while one was open for 31% of the time, Pallas kernels for 0%

commit v1 on v0

--- a/solution.py
+++ b/solution.py
@@ -5,6 +5,13 @@
 from jax.sharding import PartitionSpec as P
 
 eps = 1e-06
+
+
+def exchange_gather(value, mesh_axis, d):
+    n_dev = lax.axis_size(mesh_axis)
+    blocks = jnp.stack([value for _ in range(n_dev)])
+    blocks = lax.all_to_all(blocks, mesh_axis, split_axis=0, concat_axis=0)
+    return jnp.concatenate(blocks, axis=d)
 
 
 def with_halo(block, sides, width):
@@ -142,11 +149,10 @@
         ((("sph", "grp"), 0),),
         block_count,
     )
-    second_table = lax.all_gather(
+    second_table = exchange_gather(
         project(renewed_two, 1, address_matrix, content_matrix, rescale_factors, channel_groups),
         "grp",
-        axis=0,
-        tiled=True,
+        0,
     )
     third_table = lax.all_gather(
         project(renewed_three, 2, address_matrix, content_matrix, rescale_factors, channel_groups),

time: 176 us -> 153 us (0.87)
  blocking collectives: 52.8 us -> 24.7 us
  starting transfers between devices: 9.98 us -> 13.3 us
    all_gather x1 -> x0, blocking collectives: 22.1 us -> none  [per_device(): lax.all_gather(project(renewed_two, 1, address_matrix, content_matrix, re...]
    all_gather x1, blocking collectives: 30.7 us -> 24.7 us  [per_device(): lax.all_gather(project(renewed_three, 2, address_matrix, content_matrix,...]
    all_to_all x0 -> x1, starting transfers between devices: none -> 3.35 us  [exchange_gather(): blocks = lax.all_to_all(blocks, mesh_axis, split_axis=0, concat_axis=0)]
  transfers between devices with their start and end apart: 2 -> 3, of which waited for: 0 -> 0; matrix products, arithmetic and copies ran while one was open for 31% -> 37% of each run, Pallas kernels for 0% -> 0%
where the time goes in v1:
time: 153 us; the launch traced here: 152 us
  local copies, waits for them, and re-layouts  63.8 us (42%)
  matrix products  38.3 us (25%)
  blocking collectives  24.7 us (16%)
  starting transfers between devices  13.3 us (9%)
  other arithmetic  11.3 us (7%)
    all_gather x1, blocking collectives, per_device(): lax.all_gather(project(renewed_three, 2, address_matrix, content_matrix,...  24.7 us
    gather x3, local copies, waits for them, and re-layouts, mix_across_tiers(): key_picked = jnp.take(key_heads, tier_positions, axis=1)  22.8 us
    gather x3, local copies, waits for them, and re-layouts, mix_across_tiers(): value_picked = jnp.take(value_heads, tier_positions, axis=1)  22.8 us
    dot_general x3, matrix products, mix_across_tiers(): jnp.einsum('hbid,hbjd->hbij', queries, key_picked, preferred_element_type...  9.67 us
    unnamed x3, matrix products  7.44 us
    dot_general x3, matrix products, refresh(): jnp.dot(hidden, shrink_matrix[tier_ordinal], preferred_element_type=jnp.f...  6.3 us
    dot_general x3, matrix products, mix_across_tiers(): jnp.einsum('hbij,hbjd->hbid', weights, value_picked, preferred_element_ty...  6.02 us
    ppermute x1, starting transfers between devices, with_halo(): lax.ppermute(lax.slice_in_dim(block, 0, width, axis=dim), axis, backward)  5.95 us
  transfers between devices with their start and end apart: 3, of which 0 were waited for; matrix products, arithmetic and copies ran while one was open for 37% of the time, Pallas kernels for 0%

profile of v1, /device:TPU:1, one launch (start us, length us, event | category | flops | bytes accessed | tf_op | source)
XLA Modules:
  0.0 152.1 jit_solution(9792574985340904014)
XLA Ops:
  2.4 2.1 %fusion.35 = bf16[64,512]{1,0:T(8,128)(2,1)S(1)} fusion(bf16[3,1024,512]{2,1,0:T(8,128)(2,1)} %param.31, bf16[3,512,1024]{2,1,0:T(8,128)(2,1)} %param.30, bf16[64,512]{1,0:T(8,128)(2,1)} %param.20, f32[512]{0:T(512)S(1)} %bitcast.232, f32[64]{0:T(128)S(1)} %add_rsqrt_fusion.14), kind=kOutput, calls=%fused_computation.63 | convolution fusion | flops 134774784 | bytes 2296064 | tf_op jit(solution)/shard_map/dot_general | solution.py:55
  4.6 1.5 slice_bitcast_fusion
  8.2 4.0 %collective-permute-start = (bf16[64,1024]{1,0:T(8,128)(2,1)S(1)}, bf16[64,1024]{1,0:T(8,128)(2,1)}, u32[]{:S(2)}, u32[]{:S(2)}) collective-permute-start(bf16[64,1024]{1,0:T(8,128)(2,1)S(1)} %pad_maximum_fusion.1), channel_id=1, source_target_pairs={{0,1},{1,2},{2,3},{3,4},{4,5},{5,6},{6,7},{7,8},{8,9},{9,10},{10,1... | collective-permute-start | bytes 393224 | tf_op jit(solution)/shard_map/ppermute | solution.py:22
  12.2 6.0 %collective-permute-start.1 = (bf16[64,1024]{1,0:T(8,128)(2,1)S(1)}, bf16[64,1024]{1,0:T(8,128)(2,1)}, u32[]{:S(2)}, u32[]{:S(2)}) collective-permute-start(bf16[64,1024]{1,0:T(8,128)(2,1)S(1)} %pad_maximum_fusion.1), channel_id=1, source_target_pairs={{1,0},{2,1},{3,2},{4,3},{5,4},{6,5},{7,6},{8,7},{9,8},{10,9},{11,1... | collective-permute-start | bytes 393224 | tf_op jit(solution)/shard_map/ppermute | solution.py:25
  18.3 2.1 %fusion.36 = bf16[4,512]{1,0:T(4,128)(2,1)S(1)} fusion(bf16[3,1024,512]{2,1,0:T(8,128)(2,1)} %param.31, bf16[3,512,1024]{2,1,0:T(8,128)(2,1)} %param.30, bf16[4,512]{1,0:T(4,128)(2,1)S(1)} %copy-done.19, f32[512]{0:T(512)S(1)} %bitcast.231, f32[4]{0:T(128)S(1)} %add_rsqrt_fusion.12), kind=kOutput, calls=%fused_computation.66 | convolution fusion | flops 8423424 | bytes 2112000 | tf_op jit(solution)/shard_map/dot_general | solution.py:55
  23.3 3.3 %all-to-all-start = ((bf16[8,4,1024]{2,1,0:T(4,128)(2,1)}), bf16[8,4,1024]{2,1,0:T(4,128)(2,1)S(1)}, u32[]{:S(2)}, u32[]{:S(2)}) async-start(bf16[8,4,1024]{2,1,0:T(4,128)(2,1)} %stack.2), calls=%async_computation | async-start | bytes 131072 | tf_op jit(solution)/shard_map/all_to_all | solution.py:13
  29.5 3.3 %multiply_reduce_fusion.4 = (f32[8,1024]{1,0:T(8,128)S(1)}, f32[1024,512]{0,1}) fusion(bf16[1024,512]{0,1:T(8,128)(2,1)S(1)} %copy.136, f32[512]{0:T(512)S(1)} %bitcast.230, f32[1024]{0:T(1024)S(1)} %add_rsqrt_fusion.8, bf16[3,512,512]{2,1,0:T(8,128)(2,1)} %param.26), kind=kOutput, calls=%fused_computation.54 | convolution fusion | flops 540008448 | bytes 3708928
  35.0 2.1 %fusion.37 = bf16[2,512]{1,0:T(2,128)(2,1)S(1)} fusion(bf16[3,1024,512]{2,1,0:T(8,128)(2,1)} %param.31, bf16[3,512,1024]{2,1,0:T(8,128)(2,1)} %param.30, bf16[2,512]{1,0:T(2,128)(2,1)S(1)} %copy-done.21, f32[2]{0:T(128)S(1)} %add_rsqrt_fusion.10, f32[512]{0:T(512)S(1)} %bitcast.229), kind=kOutput, calls=%fused_computation.69 | convolution fusion | flops 4211712 | bytes 2105856 | tf_op jit(solution)/shard_map/dot_general | solution.py:55
  39.4 24.7 %all-gather = bf16[16,2,1024]{2,1,0:T(2,128)(2,1)S(1)} all-gather(bf16[1,2,1024]{2,1,0:T(2,128)(2,1)S(1)} %maximum_bitcast_fusion), channel_id=1, replica_groups=mesh['sph'=16,'grp'=8] {'sph'}, dimensions={0}, use_global_device_ids=true | all-gather | bytes 69632 | tf_op jit(solution)/shard_map/all_gather | solution.py:157
  72.0 7.6 %gather_fusion.4 = bf16[1024,8,64]{2,1,0:T(8,128)(2,1)} fusion(bf16[8,32,64]{2,0,1:T(8,128)(2,1)S(1)} %bitcast.197, s32[1024]{0:T(1024)S(1)} %broadcast_clamp_fusion), kind=kCustom, calls=%fused_computation.4.clone | custom fusion | bytes 2101248 | tf_op jit(solution)/shard_map/jit(_take)/gather | solution.py:102
  79.6 7.6 %gather_fusion.5 = bf16[1024,8,64]{2,1,0:T(8,128)(2,1)} fusion(bf16[8,32,64]{2,0,1:T(8,128)(2,1)S(1)} %bitcast.198, s32[1024]{0:T(1024)S(1)} %broadcast_clamp_fusion), kind=kCustom, calls=%fused_computation.5.clone | custom fusion | bytes 2101248 | tf_op jit(solution)/shard_map/jit(_take)/gather | solution.py:103
  87.4 7.6 %gather_fusion.2 = bf16[1024,8,64]{2,1,0:T(8,128)(2,1)} fusion(bf16[8,32,64]{2,0,1:T(8,128)(2,1)S(1)} %bitcast.199, s32[1024]{0:T(1024)S(1)} %broadcast_clamp_fusion.1), kind=kCustom, calls=%fused_computation.1.clone | custom fusion | bytes 2101248 | tf_op jit(solution)/shard_map/jit(_take)/gather | solution.py:102
  95.0 7.6 %gather_fusion.3 = bf16[1024,8,64]{2,1,0:T(8,128)(2,1)} fusion(bf16[8,32,64]{2,0,1:T(8,128)(2,1)S(1)} %bitcast.200, s32[1024]{0:T(1024)S(1)} %broadcast_clamp_fusion.1), kind=kCustom, calls=%fused_computation.3.clone | custom fusion | bytes 2101248 | tf_op jit(solution)/shard_map/jit(_take)/gather | solution.py:103
  104.4 7.6 %gather_fusion.1 = bf16[1024,8,64]{2,1,0:T(8,128)(2,1)} fusion(bf16[8,192,64]{2,0,1:T(8,128)(2,1)S(1)} %bitcast.201, s32[1024]{0:T(1024)S(1)} %broadcast_clamp_fusion.2), kind=kCustom, calls=%fused_computation.2.clone | custom fusion | bytes 2101248 | tf_op jit(solution)/shard_map/jit(_take)/gather | solution.py:103
  112.0 7.6 %gather_fusion = bf16[1024,8,64]{2,1,0:T(8,128)(2,1)} fusion(bf16[8,192,64]{2,0,1:T(8,128)(2,1)S(1)} %bitcast.202, s32[1024]{0:T(1024)S(1)} %broadcast_clamp_fusion.2), kind=kCustom, calls=%fused_computation.clone | custom fusion | bytes 2101248 | tf_op jit(solution)/shard_map/jit(_take)/gather | solution.py:102
  119.7 3.5 %select_bitcast_fusion.1 = (bf16[8,64,16,64]{3,0,2,1:T(8,128)(2,1)S(1)}, bf16[8,64,16,64]{3,0,2,1:T(8,128)(2,1)S(1)}) fusion(bf16[64,16,8,64]{3,2,1,0:T(8,128)(2,1)} %bitcast.205, pred[64,16]{1,0:T(8,128)(4,1)S(1)} %copy-done.13, bf16[64,16,8,64]{3,2,1,0:T(8,128)(2,1)} %bitcast.204), kind=kLoop, calls=%fused_computation.41 | loop fusion | flops 1048576 | bytes 4195328 | tf_op jit(solution)/shard_map/jit(_take)/select_n | solution.py:102
  124.7 1.6 %fusion.26 = bf16[8,64,16,64]{3,2,1,0:T(8,128)(2,1)S(1)} fusion(bf16[8,64,16,64]{3,0,2,1:T(8,128)(2,1)S(1)} %get-tuple-element.33, f32[8,64,16,16]{2,3,1,0:T(8,128)S(1)} %get-tuple-element.42, f32[8,64,16]{2,1,0:T(8,128)S(1)} %get-tuple-element.41, f32[8]{0:T(128)S(1)} %copy-done.20), kind=kOutput, calls=%fused_computation.59 | convolution fusion | flops 17694720 | bytes 2654240 | tf_op jit(solution)/shard_map/hbij,hbjd->hbid/dot_general | solution.py:113
  127.8 2.3 %multiply_reduce_fusion.2 = (f32[8,1024]{1,0:T(8,128)S(1)}, f32[1024,512]{0,1:S(1)}) fusion(f32[1024,512]{0,1:T(8,128)S(1)} %get-tuple-element.46, f32[512]{0:T(512)S(1)} %bitcast.222, f32[1024]{0:T(1024)S(1)} %add_rsqrt_fusion.6, bf16[3,512,512]{2,1,0:T(8,128)(2,1)} %param.26), kind=kOutput, calls=%fused_computation.49 | convolution fusion | flops 539484160 | bytes 4757504
  131.5 4.3 %fusion.1 = (f32[8,64,16]{2,1,0:T(8,128)S(1)}, f32[8,64,16,16]{2,3,1,0:T(8,128)S(1)}) fusion(f32[8]{0:T(128)S(1)} %copy-done.23, bf16[8,64,16,64]{3,2,1,0:T(8,128)(2,1)S(1)} %bitcast.207, bf16[64,16,8,64]{3,2,1,0:T(8,128)(2,1)} %bitcast.212, pred[64,16]{1,0:T(8,128)(4,1)S(1)} %copy-done.18), kind=kOutput, calls=%fused_computation.13 | convolution fusion | flops 17555456 | bytes 2655264 | tf_op jit(solution)/shard_map/hbid,hbjd->hbij/dot_general | solution.py:104
  135.8 2.3 %fusion.29 = bf16[8,64,16,64]{3,2,1,0:T(8,128)(2,1)S(1)} fusion(bf16[64,16,8,64]{3,2,1,0:T(8,128)(2,1)S(1)} %bitcast.211, pred[64,16]{1,0:T(8,128)(4,1)S(1)} %copy-done.18, f32[8,64,16,16]{2,3,1,0:T(8,128)S(1)} %get-tuple-element.50, f32[8,64,16]{2,1,0:T(8,128)S(1)} %get-tuple-element.49, f32[8]{0:T(128)S(1)} %copy-done.23), kind=kOutput, calls=%fused_computation.60 | convolution fusion | flops 18219008 | bytes 2655264 | tf_op jit(solution)/shard_map/hbij,hbjd->hbid/dot_general | solution.py:113
  139.5 1.9 %multiply_reduce_fusion = (f32[8,1024]{1,0:T(8,128)S(1)}, f32[1024,512]{0,1:S(1)}) fusion(f32[1024,512]{0,1:T(8,128)S(1)} %get-tuple-element.54, f32[512]{0:T(512)S(1)} %bitcast.221, f32[1024]{0:T(1024)S(1)} %add_rsqrt_fusion.4, bf16[3,512,512]{2,1,0:T(8,128)(2,1)} %param.26), kind=kOutput, calls=%fused_computation.44 | convolution fusion | flops 539484160 | bytes 4757504
  141.7 1.8 %copy.169 = bf16[8,1024,64]{2,1,0:T(8,128)(2,1)} copy(bf16[8,1024,64]{1,2,0:T(8,128)(2,1)S(1)} %multiply_convert_fusion) | data formatting | bytes 2097152 | tf_op jit(solution)/shard_map/convert_element_type | solution.py:93
  143.5 3.9 %fusion.2 = (f32[8,64,16]{2,1,0:T(8,128)S(1)}, f32[8,64,16,16]{2,3,1,0:T(8,128)S(1)}) fusion(f32[8]{0:T(128)S(1)} %copy-done.22, bf16[8,64,16,64]{3,2,1,0:T(8,128)(2,1)} %bitcast.206, bf16[64,16,8,64]{3,2,1,0:T(8,128)(2,1)} %bitcast.210, pred[64,16]{1,0:T(8,128)(4,1)S(1)} %copy.170), kind=kOutput, calls=%fused_computation.14 | convolution fusion | flops 17555456 | bytes 2655264 | tf_op jit(solution)/shard_map/hbid,hbjd->hbij/dot_general | solution.py:104
  147.4 2.1 %fusion.32 = bf16[8,64,16,64]{3,2,1,0:T(8,128)(2,1)S(1)} fusion(bf16[64,16,8,64]{3,2,1,0:T(8,128)(2,1)S(1)} %bitcast.209, pred[64,16]{1,0:T(8,128)(4,1)S(1)} %copy.170, f32[8,64,16,16]{2,3,1,0:T(8,128)S(1)} %get-tuple-element.58, f32[8,64,16]{2,1,0:T(8,128)S(1)} %get-tuple-element.57, f32[8]{0:T(128)S(1)} %copy-done.22), kind=kOutput, calls=%fused_computation.61 | convolution fusion | flops 18219008 | bytes 2655264 | tf_op jit(solution)/shard_map/hbij,hbjd->hbid/dot_general | solution.py:113
  (138 shorter events, 33.0 us)
Async XLA Ops:
  6.1 12.1 %copy-start.19 = (bf16[4,512]{1,0:T(4,128)(2,1)S(1)}, bf16[4,512]{1,0:T(4,128)(2,1)}, u32[]{:S(2)}) copy-start(bf16[4,512]{1,0:T(4,128)(2,1)} %param.21) | copy-start | bytes 12292
  8.2 94.4 %collective-permute-start = (bf16[64,1024]{1,0:T(8,128)(2,1)S(1)}, bf16[64,1024]{1,0:T(8,128)(2,1)}, u32[]{:S(2)}, u32[]{:S(2)}) collective-permute-start(bf16[64,1024]{1,0:T(8,128)(2,1)S(1)} %pad_maximum_fusion.1), channel_id=1, source_target_pairs={{0,1},{1,2},{2,3},{3,4},{4,5},{5,6},{6,7},{7,8},{8,9},{9,10},{10,1... | collective-permute-start | bytes 393224 | tf_op jit(solution)/shard_map/ppermute | solution.py:22
  12.2 90.4 %collective-permute-start.1 = (bf16[64,1024]{1,0:T(8,128)(2,1)S(1)}, bf16[64,1024]{1,0:T(8,128)(2,1)}, u32[]{:S(2)}, u32[]{:S(2)}) collective-permute-start(bf16[64,1024]{1,0:T(8,128)(2,1)S(1)} %pad_maximum_fusion.1), channel_id=1, source_target_pairs={{1,0},{2,1},{3,2},{4,3},{5,4},{6,5},{7,6},{8,7},{9,8},{10,9},{11,1... | collective-permute-start | bytes 393224 | tf_op jit(solution)/shard_map/ppermute | solution.py:25
  18.3 8.4 %copy-start.14 = (s32[64,16]{0,1:T(8,128)S(1)}, s32[64,16]{0,1:T(8,128)}, u32[]{:S(2)}) copy-start(s32[64,16]{0,1:T(8,128)} %param.25) | copy-start | bytes 12292
  18.3 9.6 %copy-start.16 = (s32[64,16]{0,1:T(8,128)S(1)}, s32[64,16]{0,1:T(8,128)}, u32[]{:S(2)}) copy-start(s32[64,16]{0,1:T(8,128)} %param.23) | copy-start | bytes 12292
  18.3 10.3 %copy-start.8 = (bf16[1024,512]{1,0:T(8,128)(2,1)S(1)}, bf16[1024,512]{1,0:T(8,128)(2,1)}, u32[]{:S(2)}) copy-start(bf16[1024,512]{1,0:T(8,128)(2,1)} %param.19) | copy-start | bytes 3145732
  23.3 63.9 %all-to-all-start = ((bf16[8,4,1024]{2,1,0:T(4,128)(2,1)}), bf16[8,4,1024]{2,1,0:T(4,128)(2,1)S(1)}, u32[]{:S(2)}, u32[]{:S(2)}) async-start(bf16[8,4,1024]{2,1,0:T(4,128)(2,1)} %stack.2), calls=%async_computation | async-start | bytes 131072 | tf_op jit(solution)/shard_map/all_to_all | solution.py:13
  29.2 3.6 %copy-start = (bf16[1024,512]{0,1:T(8,128)(2,1)}, bf16[1024,512]{0,1:T(8,128)(2,1)S(1)}, u32[]{:S(2)}) copy-start(bf16[1024,512]{0,1:T(8,128)(2,1)S(1)} %copy.136) | copy-start | bytes 3145732
  29.4 3.4 %copy-start.7 = (bf16[3,512,512]{2,1,0:T(8,128)(2,1)S(1)}, bf16[3,512,512]{2,1,0:T(8,128)(2,1)}, u32[]{:S(2)}) copy-start(bf16[3,512,512]{2,1,0:T(8,128)(2,1)} %param.29) | copy-start | bytes 4718596
  32.8 2.0 %copy-start.21 = (bf16[2,512]{1,0:T(2,128)(2,1)S(1)}, bf16[2,512]{1,0:T(2,128)(2,1)}, u32[]{:S(2)}) copy-start(bf16[2,512]{1,0:T(2,128)(2,1)} %param.22) | copy-start | bytes 6148
  35.0 30.6 %copy-start.4 = (f32[1024,512]{0,1:S(1)}, f32[1024,512]{0,1}, u32[]{:S(2)}) copy-start(f32[1024,512]{0,1} %get-tuple-element.40) | copy-start | bytes 6291460
  65.9 5.2 %copy-start.12 = (bf16[32,512]{1,0:T(8,128)(2,1)S(1)}, bf16[32,512]{1,0:T(8,128)(2,1)}, u32[]{:S(2)}) copy-start(bf16[32,512]{1,0:T(8,128)(2,1)} %get-tuple-element.19) | copy-start | bytes 98308
  112.0 7.6 %copy-start.13 = (pred[64,16]{1,0:T(8,128)(4,1)S(1)}, pred[64,16]{1,0:T(8,128)(4,1)}, u32[]{:S(2)}) copy-start(pred[64,16]{1,0:T(8,128)(4,1)} %copy.140) | copy-start | bytes 3076
  119.7 3.5 %copy-start.20 = (f32[8]{0:T(128)S(1)}, f32[8]{0:T(128)}, u32[]{:S(2)}) copy-start(f32[8]{0:T(128)} %get-tuple-element.35) | copy-start | bytes 100
  124.7 1.7 %copy-start.1 = (bf16[1024,512]{0,1:T(8,128)(2,1)S(1)}, bf16[1024,512]{0,1:T(8,128)(2,1)}, u32[]{:S(2)}) copy-start(bf16[1024,512]{0,1:T(8,128)(2,1)} %copy-done) | copy-start | bytes 3145732
  124.7 1.7 %copy-start.11 = (bf16[1,512,512]{2,1,0:T(8,128)(2,1)S(1)}, bf16[1,512,512]{2,1,0:T(8,128)(2,1)}, u32[]{:S(2)}) copy-start(bf16[1,512,512]{2,1,0:T(8,128)(2,1)} %get-tuple-element.12) | copy-start | bytes 1572868
  126.4 1.4 copy-start.15
  127.7 2.3 %copy-start.2 = (f32[1024,512]{0,1:T(8,128)}, f32[1024,512]{0,1:T(8,128)S(1)}, u32[]{:S(2)}) copy-start(f32[1024,512]{0,1:T(8,128)S(1)} %get-tuple-element.46) | copy-start | bytes 6291460
  131.5 4.3 %copy-start.6 = (bf16[1024,8,64]{2,1,0:T(8,128)(2,1)S(1)}, bf16[1024,8,64]{2,1,0:T(8,128)(2,1)}, u32[]{:S(2)}) copy-start(bf16[1024,8,64]{2,1,0:T(8,128)(2,1)} %gather_fusion.3) | copy-start | bytes 3145732
  135.8 2.3 %copy-start.3 = (f32[1024,512]{0,1:T(8,128)S(1)}, f32[1024,512]{0,1:T(8,128)}, u32[]{:S(2)}) copy-start(f32[1024,512]{0,1:T(8,128)} %copy-done.2) | copy-start | bytes 6291460
  135.8 2.3 %copy-start.10 = (bf16[1,512,512]{2,1,0:T(8,128)(2,1)S(1)}, bf16[1,512,512]{2,1,0:T(8,128)(2,1)}, u32[]{:S(2)}) copy-start(bf16[1,512,512]{2,1,0:T(8,128)(2,1)} %get-tuple-element.13) | copy-start | bytes 1572868
  141.7 1.8 %copy-start.22 = (f32[8]{0:T(128)S(1)}, f32[8]{0:T(128)}, u32[]{:S(2)}) copy-start(f32[8]{0:T(128)} %get-tuple-element.34) | copy-start | bytes 100
  143.5 3.9 %copy-start.5 = (bf16[1024,8,64]{2,1,0:T(8,128)(2,1)S(1)}, bf16[1024,8,64]{2,1,0:T(8,128)(2,1)}, u32[]{:S(2)}) copy-start(bf16[1024,8,64]{2,1,0:T(8,128)(2,1)} %gather_fusion.5) | copy-start | bytes 3145732
  147.4 2.1 %copy-start.9 = (bf16[1,512,512]{2,1,0:T(8,128)(2,1)S(1)}, bf16[1,512,512]{2,1,0:T(8,128)(2,1)}, u32[]{:S(2)}) copy-start(bf16[1,512,512]{2,1,0:T(8,128)(2,1)} %get-tuple-element.11) | copy-start | bytes 1572868
  (3 other events, 3.5 us)
